TPU v7x, 128 devices: a whole 4x4x4 slice. The times are simulated.
128 devices in a mesh: sx: 8 (over y, core), sy: 16 (over x, z).
Axes of the slice: x: 4, y: 4, z: 4, core: 2. Of those that a mesh axis runs over, the one named last changes fastest.
Arguments:
- loads: float32 [8, 16, 1536, 256], P('sx', 'sy')
- schur_flex: float32 [8, 16, 1536, 1536], P('sx', 'sy'), as said below
- dirichlet: float32 [8, 16, 1536, 1536], P('sx', 'sy'), as said below
- coupling: float32 [8, 16, 16, 1536], P('sx', 'sy'), may hold values from -0.3125 to 0.3125
- corner_index: int32 [8, 16, 16], P('sx', 'sy'), may hold values from 0 to 512, as said below
- face_lists: int32 [8, 16, 4, 384], P('sx', 'sy'), may hold values from 0 to 383, as said below
- coarse_inverse: float32 [512, 512], P(('sx', 'sy')), as said below
Outputs:
- multipliers: float32 [8, 16, 1536, 256], P('sx', 'sy')
- residual: float32 [8, 16, 1536, 256], P('sx', 'sy')
Inputs may be any that keep to these rules, and one draw needn't show every extreme that they name: `corner_index`: each subdomain lists 4 coarse dofs for each of its four corners; 512 marks a corner on the clamped edges of the panel, which has no coarse dof; every coarse dof below 512 is named by some subdomain. `face_lists`: each face's list is a permutation of the 384 dofs of the facing face; the facing lists of two neighbouring subdomains are inverse permutations. `schur_flex`: symmetric positive definite for every subdomain. `dirichlet`: symmetric positive definite for every subdomain. `coarse_inverse`: symmetric positive definite.
All inputs are finite; a program needn't handle non-finite values.
Results may differ from a plain program's by a relative error of at most 0.00017.
Values sent between devices are 32-bit elements; how exact they have to be, the bound alone decides.
A program may use at most 128 MiB of HBM per device.

v0:
```python
import jax
import jax.numpy as jnp
from jax import lax
from jax.sharding import PartitionSpec as P

HIGH = lax.Precision.HIGH
HIGHEST = lax.Precision.HIGHEST


def shifted(block, axis, distance):
    devices = range(lax.axis_size(axis))
    route = [(i - distance, i) for i in devices if i - distance in devices]
    return lax.ppermute(block, axis, route)


def facing(faces):
    return (
        shifted(faces[1], "sx", 1),
        shifted(faces[0], "sx", -1),
        shifted(faces[3], "sy", 1),
        shifted(faces[2], "sy", -1),
    )


def jump(field, match):
    size = field.shape[0] // 4
    faces = [field[f * size : (f + 1) * size] for f in range(4)]
    received = facing(faces)
    return jnp.concatenate(
        [faces[f] - jnp.dot(match[f], received[f], precision=HIGHEST) for f in range(4)], axis=0
    )


def inner(first, second):
    return jnp.sum(first * second, axis=0)


def shards(loads, schur_flex, dirichlet, coupling, corner_index, face_lists, coarse_inverse):
    flex_mat = schur_flex[0, 0]
    prec_mat = dirichlet[0, 0]
    coupling_mat = coupling[0, 0]
    corners = corner_index[0, 0]
    face_index = face_lists[0, 0]
    ncoarse = coarse_inverse.shape[1]
    ncl = corners.shape[0]
    size = face_index.shape[1]
    sx = lax.axis_index("sx")
    sy = lax.axis_index("sy")
    inside = jnp.stack([sx > 0, sx < lax.axis_size("sx") - 1, sy > 0, sy < lax.axis_size("sy") - 1])
    scale = jnp.repeat(1.0 + inside.astype(jnp.float32), size)[:, None]
    match = (face_index[:, :, None] == jnp.arange(size, dtype=jnp.int32)[None, None, :]).astype(
        jnp.float32
    )
    inverse = lax.all_gather(coarse_inverse, ("sx", "sy"), axis=0, tiled=True)
    slots = jnp.concatenate([corners, jnp.arange(ncoarse + 1, ncoarse + 4, dtype=jnp.int32)])
    place = (slots[None, :] == jnp.arange(ncoarse + 8, dtype=jnp.int32)[:, None]).astype(
        jnp.float32
    )
    coarse_ids = jnp.arange(ncoarse, dtype=jnp.float32)[None, :]
    own = corners.astype(jnp.float32)
    parts = [coupling_mat[:, f * size : (f + 1) * size].T for f in range(4)]
    tagged = [jnp.concatenate([part, jnp.broadcast_to(own, (8, ncl))], axis=0) for part in parts]
    pick = (own[:, None] == coarse_ids).astype(jnp.float32)
    columns = []
    for f, got in enumerate(facing(tagged)):
        their_pick = (got[size][:, None] == coarse_ids).astype(jnp.float32)
        theirs = jnp.dot(match[f], got[:size], precision=HIGHEST)
        columns.append(
            jnp.dot(parts[f], pick, precision=HIGHEST)
            - jnp.dot(theirs, their_pick, precision=HIGHEST)
        )
    coupling_jump = jnp.concatenate(columns, axis=0)

    def reduced(local_load, *rows):
        rows = list(rows) + [jnp.zeros_like(rows[0])] * (3 - len(rows))
        block = jnp.concatenate([local_load] + [row[None] for row in rows], axis=0)
        total = lax.psum(jnp.dot(place, block, precision=HIGHEST), ("sx", "sy"))
        return (total[:ncoarse], total[ncoarse + 1], total[ncoarse + 2], total[ncoarse + 3])

    def coarse(rhs):
        sol = jnp.dot(inverse, rhs, precision=HIGHEST)
        return (jnp.dot(coupling_jump, sol, precision=HIGHEST), inner(rhs, sol))

    def precondition(residual):
        spread = scale * residual
        applied = jnp.dot(prec_mat, spread, precision=HIGH)
        return (0.5 * jump(applied, match), 0.5 * inner(spread, applied))

    def flexible(direction):
        spread = scale * direction
        return (
            spread,
            jnp.dot(flex_mat, spread, precision=HIGH),
            jnp.dot(coupling_mat, spread, precision=HIGH),
        )

    residual = jump(loads[0, 0], match)
    direction, dot_part = precondition(residual)
    spread, flexed, load = flexible(direction)
    rhs, res_dot, energy, _ = reduced(load, dot_part, inner(spread, flexed))
    image = jump(flexed, match)
    correction, coarse_energy = coarse(rhs)
    step = res_dot / (energy + coarse_energy)
    residual = residual - step * (image + correction)
    multipliers = step * direction
    precond, dot_part = precondition(residual)
    spread, new_flexed, load = flexible(precond)
    new_rhs, new_dot, new_energy, cross = reduced(
        load, dot_part, inner(spread, new_flexed), inner(spread, flexed)
    )
    new_image = jump(new_flexed, match)
    beta = new_dot / res_dot
    rhs = new_rhs + beta * rhs
    energy = new_energy + beta * (2.0 * cross + beta * energy)
    correction, coarse_energy = coarse(rhs)
    step = new_dot / (energy + coarse_energy)
    multipliers = multipliers + step * (precond + beta * direction)
    residual = residual - step * (new_image + beta * image + correction)
    return (multipliers[None, None], residual[None, None])


def solution(mesh):
    return jax.shard_map(
        shards,
        mesh=mesh,
        in_specs=(
            P("sx", "sy", None, None),
            P("sx", "sy", None, None),
            P("sx", "sy", None, None),
            P("sx", "sy", None, None),
            P("sx", "sy", None),
            P("sx", "sy", None, None),
            P(("sx", "sy"), None),
        ),
        out_specs=(P("sx", "sy", None, None), P("sx", "sy", None, None)),
        check_vma=False,
    )
```

profile of v0, /device:TPU:1, one launch (start us, length us, event | category | flops | bytes accessed | tf_op | source)
XLA Modules:
  0.0 480.3 jit_solution(9736556489605518894)
XLA Ops:
  9.5 4.6 collective-permute-start.12
  16.0 3.5 collective-permute-start.14
  23.5 3.9 collective-permute-start
  36.4 4.3 collective-permute-start.2
  49.7 5.8 %collective-permute-done.3 = f32[384,256]{1,0:T(8,128)S(1)} collective-permute-done((f32[384,256]{1,0:T(8,128)S(1)}, f32[384,256]{1,0:T(8,128)S(1)}, u32[]{:S(2)}, u32[]{:S(2)}) %collective-permute-start.3) | collective-permute-done | bytes 393248 | tf_op jit(solution)/shard_map/ppermute | solution.py:13
  56.1 4.1 multiply_reduce_fusion.4
  60.4 4.6 collective-permute-start.4
  66.4 3.4 collective-permute-start.6
  74.2 4.1 collective-permute-done.6
  78.8 3.3 collective-permute-done.7
  83.3 4.2 multiply_reduce_fusion.3
  88.4 4.1 collective-permute-start.8
  92.5 5.6 %collective-permute-start.10 = (f32[384,256]{1,0:T(8,128)}, f32[384,256]{1,0:T(8,128)}, u32[]{:S(2)}, u32[]{:S(2)}) collective-permute-start(f32[384,256]{1,0:T(8,128)} %get-tuple-element.13), channel_id=1, source_target_pairs={{0,1},{1,2},{2,3},{3,4},{4,5},{5,6},{6,7},{7,8},{8,9},{9,10},{10,1... | collective-permute-start | bytes 1179656 | tf_op jit(solution)/shard_map/ppermute | solution.py:13
  116.8 134.1 %all-reduce.3.cloned.1.call-done = f32[520,256]{1,0:T(8,128)} async-done(((f32[520,256]{1,0:T(8,128)}), f32[520,256]{1,0:T(8,128)}) %all-reduce.3.cloned.1.call-update) | async-done | bytes 532496 | tf_op jit(solution)/shard_map/psum | solution.py:77
  251.0 3.7 fusion.36
  258.8 5.7 %fusion.9 = f32[1536,256]{1,0:T(8,128)S(1)} fusion(f32[256,512]{1,0:T(8,128)} %fusion.36, f32[384,512]{1,0:T(8,128)} %convolution_subtract_fusion, f32[384,512]{1,0:T(8,128)} %convolution_subtract_fusion.1, f32[384,512]{1,0:T(8,128)} %convolution_subtract_fusion.2, f32[384,512]{1,0:T(8,128)} %convolution_subtract_fusion.3, ...), kind=kOutput, calls=%fused_computation.11 | convolution fusion | flops 2421817344 | bytes 8389632 | tf_op jit(solution)/shard_map/dot_general | solution.py:82
  264.6 7.4 %multiply_reduce_fusion.2 = (f32[256]{0:T(256)S(1)}, f32[1536,256]{1,0:T(8,128)S(1)}) fusion(f32[1536,256]{1,0:T(8,128)S(1)} %fusion.9, f32[1536]{0:T(1024)S(1)} %mul.194, f32[1,1,1536,1536]{3,2,1,0:T(8,128)} %param.9), kind=kOutput, calls=%fused_computation.34 | convolution fusion | flops 3625451264 | bytes 12590080 | tf_op jit(solution)/shard_map/dot_general | solution.py:86
  281.6 4.1 collective-permute-done.18
  290.7 5.8 %multiply_reduce_fusion.1 = (f32[256]{0:T(256)S(1)}, f32[256]{0:T(256)S(1)}, f32[1536,256]{1,0:T(8,128)}) fusion(f32[1536]{0:T(1024)S(1)} %broadcast_multiply_fusion, f32[384,256]{1,0:T(8,128)S(1)} %convolution_subtract_fusion.8, f32[384,256]{1,0:T(8,128)S(1)} %convolution_subtract_fusion.9, f32[384,256]{1,0:T(8,128)S(1)} %convolution_subtract_fusion.10, ...), kind=kOutput, calls=%fused_computation.33 | convolution fusion | flops 3628596736 | bytes 14163968 | tf_op jit(solution)/shard_map/dot_general | solution.py:93
  299.5 3.8 collective-permute-start.20
  303.3 3.9 collective-permute-start.22
  310.6 139.0 %all-reduce.5.cloned.1.call-done = f32[520,256]{1,0:T(8,128)} async-done(((f32[520,256]{1,0:T(8,128)}), f32[520,256]{1,0:T(8,128)}) %all-reduce.5.cloned.1.call-update) | async-done | bytes 532496 | tf_op jit(solution)/shard_map/psum | solution.py:77
  450.4 3.9 fusion.40
  468.3 5.2 %fusion.29 = f32[1,1,1536,256]{3,2,1,0:T(8,128)} fusion(f32[1536,256]{1,0:T(8,128)S(1)} %copy-done.23, f32[384,256]{1,0:T(8,128)S(1)} %convolution_subtract_fusion.4, f32[384,256]{1,0:T(8,128)S(1)} %convolution_subtract_fusion.5, f32[384,256]{1,0:T(8,128)S(1)} %convolution_subtract_fusion.6, f32[384,256]{1,0:T(8,128)S(1)} %convolution_subtract_fusion.7, ...), kind=kOutput, calls=%fused_computation.31 | convolution fusion | flops 2422603776 | bytes 9963520 | tf_op jit(solution)/shard_map/dot_general | solution.py:82
  (197 shorter events, 93.1 us)
Async XLA Ops:
  7.2 108.1 %all-gather.3.cloned.1.call-start = ((), (), s32[]{:S(2)}) async-start(), calls=%async_computation.2 | async-start | bytes 1056768 | tf_op jit(solution)/shard_map/all_gather | solution.py:54
  7.9 243.1 %all-reduce.3.cloned.1.call-start = ((), (), s32[]{:S(2)}) async-start(), calls=%async_computation | async-start | bytes 1064960 | tf_op jit(solution)/shard_map/psum | solution.py:77
  9.5 36.9 %collective-permute-start.12 = (f32[392,16]{0,1:T(8,128)S(1)}, f32[392,16]{0,1:T(8,128)S(1)}, u32[]{:S(2)}, u32[]{:S(2)}) collective-permute-start(f32[392,16]{0,1:T(8,128)S(1)} %get-tuple-element.28), channel_id=1, source_target_pairs={{0,16},{16,32},{32,48},{48,64},{64,80},{80,96},{96,112},{1,17},{17... | collective-permute-start | bytes 75272 | tf_op jit(solution)/shard_map/ppermute | solution.py:13
  14.1 28.5 %collective-permute-start.13 = (f32[392,16]{0,1:T(8,128)S(1)}, f32[392,16]{0,1:T(8,128)S(1)}, u32[]{:S(2)}, u32[]{:S(2)}) collective-permute-start(f32[392,16]{0,1:T(8,128)S(1)} %get-tuple-element.29), channel_id=1, source_target_pairs={{16,0},{32,16},{48,32},{64,48},{80,64},{96,80},{112,96},{17,1},{33... | collective-permute-start | bytes 75272 | tf_op jit(solution)/shard_map/ppermute | solution.py:13
  16.0 20.4 %collective-permute-start.14 = (f32[392,16]{0,1:T(8,128)S(1)}, f32[392,16]{0,1:T(8,128)S(1)}, u32[]{:S(2)}, u32[]{:S(2)}) collective-permute-start(f32[392,16]{0,1:T(8,128)S(1)} %get-tuple-element.30), channel_id=1, source_target_pairs={{0,1},{1,2},{2,3},{3,4},{4,5},{5,6},{6,7},{7,8},{8,9},{9,10},{10,1... | collective-permute-start | bytes 75272 | tf_op jit(solution)/shard_map/ppermute | solution.py:13
  19.6 11.7 %collective-permute-start.15 = (f32[392,16]{0,1:T(8,128)S(1)}, f32[392,16]{0,1:T(8,128)S(1)}, u32[]{:S(2)}, u32[]{:S(2)}) collective-permute-start(f32[392,16]{0,1:T(8,128)S(1)} %get-tuple-element.31), channel_id=1, source_target_pairs={{1,0},{2,1},{3,2},{4,3},{5,4},{6,5},{7,6},{8,7},{9,8},{10,9},{11,1... | collective-permute-start | bytes 75272 | tf_op jit(solution)/shard_map/ppermute | solution.py:13
  23.5 23.4 %collective-permute-start = (f32[384,256]{1,0:T(8,128)}, f32[384,256]{1,0:T(8,128)}, u32[]{:S(2)}, u32[]{:S(2)}) collective-permute-start(f32[384,256]{1,0:T(8,128)} %get-tuple-element.20), channel_id=1, source_target_pairs={{0,16},{16,32},{32,48},{48,64},{64,80},{80,96},{96,112},{1,17},{17... | collective-permute-start | bytes 1179656 | tf_op jit(solution)/shard_map/ppermute | solution.py:13
  31.2 17.3 %collective-permute-start.1 = (f32[384,256]{1,0:T(8,128)}, f32[384,256]{1,0:T(8,128)S(1)}, u32[]{:S(2)}, u32[]{:S(2)}) collective-permute-start(f32[384,256]{1,0:T(8,128)} %get-tuple-element.21), channel_id=1, source_target_pairs={{16,0},{32,16},{48,32},{64,48},{80,64},{96,80},{112,96},{17,1},{33... | collective-permute-start | bytes 1179656 | tf_op jit(solution)/shard_map/ppermute | solution.py:13
  36.4 12.7 %collective-permute-start.2 = (f32[384,256]{1,0:T(8,128)}, f32[384,256]{1,0:T(8,128)S(1)}, u32[]{:S(2)}, u32[]{:S(2)}) collective-permute-start(f32[384,256]{1,0:T(8,128)} %get-tuple-element.22), channel_id=1, source_target_pairs={{0,1},{1,2},{2,3},{3,4},{4,5},{5,6},{6,7},{7,8},{8,9},{9,10},{10,1... | collective-permute-start | bytes 1179656 | tf_op jit(solution)/shard_map/ppermute | solution.py:13
  42.6 12.9 %collective-permute-start.3 = (f32[384,256]{1,0:T(8,128)S(1)}, f32[384,256]{1,0:T(8,128)S(1)}, u32[]{:S(2)}, u32[]{:S(2)}) collective-permute-start(f32[384,256]{1,0:T(8,128)S(1)} %copy-done.29), channel_id=1, source_target_pairs={{1,0},{2,1},{3,2},{4,3},{5,4},{6,5},{7,6},{8,7},{9,8},{10,9},{11,1... | collective-permute-start | bytes 1179656 | tf_op jit(solution)/shard_map/ppermute | solution.py:13
  60.4 13.2 %collective-permute-start.4 = (f32[384,256]{1,0:T(8,128)S(1)}, f32[384,256]{1,0:T(8,128)S(1)}, u32[]{:S(2)}, u32[]{:S(2)}) collective-permute-start(f32[384,256]{1,0:T(8,128)S(1)} %get-tuple-element.16), channel_id=1, source_target_pairs={{0,16},{16,32},{32,48},{48,64},{64,80},{80,96},{96,112},{1,17},{17... | collective-permute-start | bytes 1179656 | tf_op jit(solution)/shard_map/ppermute | solution.py:13
  66.4 11.9 %collective-permute-start.6 = (f32[384,256]{1,0:T(8,128)S(1)}, f32[384,256]{1,0:T(8,128)S(1)}, u32[]{:S(2)}, u32[]{:S(2)}) collective-permute-start(f32[384,256]{1,0:T(8,128)S(1)} %get-tuple-element.17), channel_id=1, source_target_pairs={{0,1},{1,2},{2,3},{3,4},{4,5},{5,6},{6,7},{7,8},{8,9},{9,10},{10,1... | collective-permute-start | bytes 1179656 | tf_op jit(solution)/shard_map/ppermute | solution.py:13
  69.8 12.4 %collective-permute-start.7 = (f32[384,256]{1,0:T(8,128)S(1)}, f32[384,256]{1,0:T(8,128)S(1)}, u32[]{:S(2)}, u32[]{:S(2)}) collective-permute-start(f32[384,256]{1,0:T(8,128)S(1)} %get-tuple-element.18), channel_id=1, source_target_pairs={{1,0},{2,1},{3,2},{4,3},{5,4},{6,5},{7,6},{8,7},{9,8},{10,9},{11,1... | collective-permute-start | bytes 1179656 | tf_op jit(solution)/shard_map/ppermute | solution.py:13
  71.1 11.6 %collective-permute-start.5 = (f32[384,256]{1,0:T(8,128)S(1)}, f32[384,256]{1,0:T(8,128)S(1)}, u32[]{:S(2)}, u32[]{:S(2)}) collective-permute-start(f32[384,256]{1,0:T(8,128)S(1)} %get-tuple-element.19), channel_id=1, source_target_pairs={{16,0},{32,16},{48,32},{64,48},{80,64},{96,80},{112,96},{17,1},{33... | collective-permute-start | bytes 1179656 | tf_op jit(solution)/shard_map/ppermute | solution.py:13
  88.4 15.0 %collective-permute-start.8 = (f32[384,256]{1,0:T(8,128)}, f32[384,256]{1,0:T(8,128)}, u32[]{:S(2)}, u32[]{:S(2)}) collective-permute-start(f32[384,256]{1,0:T(8,128)} %get-tuple-element.12), channel_id=1, source_target_pairs={{0,16},{16,32},{32,48},{48,64},{64,80},{80,96},{96,112},{1,17},{17... | collective-permute-start | bytes 1179656 | tf_op jit(solution)/shard_map/ppermute | solution.py:13
  92.5 13.6 %collective-permute-start.10 = (f32[384,256]{1,0:T(8,128)}, f32[384,256]{1,0:T(8,128)}, u32[]{:S(2)}, u32[]{:S(2)}) collective-permute-start(f32[384,256]{1,0:T(8,128)} %get-tuple-element.13), channel_id=1, source_target_pairs={{0,1},{1,2},{2,3},{3,4},{4,5},{5,6},{6,7},{7,8},{8,9},{9,10},{10,1... | collective-permute-start | bytes 1179656 | tf_op jit(solution)/shard_map/ppermute | solution.py:13
  98.1 12.5 %collective-permute-start.11 = (f32[384,256]{1,0:T(8,128)S(1)}, f32[384,256]{1,0:T(8,128)}, u32[]{:S(2)}, u32[]{:S(2)}) collective-permute-start(f32[384,256]{1,0:T(8,128)S(1)} %get-tuple-element.14), channel_id=1, source_target_pairs={{1,0},{2,1},{3,2},{4,3},{5,4},{6,5},{7,6},{8,7},{9,8},{10,9},{11,1... | collective-permute-start | bytes 1179656 | tf_op jit(solution)/shard_map/ppermute | solution.py:13
  99.4 13.6 %collective-permute-start.9 = (f32[384,256]{1,0:T(8,128)S(1)}, f32[384,256]{1,0:T(8,128)}, u32[]{:S(2)}, u32[]{:S(2)}) collective-permute-start(f32[384,256]{1,0:T(8,128)S(1)} %get-tuple-element.15), channel_id=1, source_target_pairs={{16,0},{32,16},{48,32},{64,48},{80,64},{96,80},{112,96},{17,1},{33... | collective-permute-start | bytes 1179656 | tf_op jit(solution)/shard_map/ppermute | solution.py:13
  103.2 346.4 %all-reduce.5.cloned.1.call-start = ((), (), s32[]{:S(2)}) async-start(), calls=%async_computation.1 | async-start | bytes 1064960 | tf_op jit(solution)/shard_map/psum | solution.py:77
  277.3 12.2 %collective-permute-start.19 = (f32[384,256]{1,0:T(8,128)S(1)}, f32[384,256]{1,0:T(8,128)S(1)}, u32[]{:S(2)}, u32[]{:S(2)}) collective-permute-start(f32[384,256]{1,0:T(8,128)S(1)} %get-tuple-element.10), channel_id=1, source_target_pairs={{1,0},{2,1},{3,2},{4,3},{5,4},{6,5},{7,6},{8,7},{9,8},{10,9},{11,1... | collective-permute-start | bytes 1179656 | tf_op jit(solution)/shard_map/ppermute | solution.py:13
  299.5 162.1 %collective-permute-start.20 = (f32[384,256]{1,0:T(8,128)}, f32[384,256]{1,0:T(8,128)}, u32[]{:S(2)}, u32[]{:S(2)}) collective-permute-start(f32[384,256]{1,0:T(8,128)} %get-tuple-element.4), channel_id=1, source_target_pairs={{0,16},{16,32},{32,48},{48,64},{64,80},{80,96},{96,112},{1,17},{17... | collective-permute-start | bytes 1179656 | tf_op jit(solution)/shard_map/ppermute | solution.py:13
  303.3 160.0 %collective-permute-start.22 = (f32[384,256]{1,0:T(8,128)}, f32[384,256]{1,0:T(8,128)}, u32[]{:S(2)}, u32[]{:S(2)}) collective-permute-start(f32[384,256]{1,0:T(8,128)} %get-tuple-element.5), channel_id=1, source_target_pairs={{0,1},{1,2},{2,3},{3,4},{4,5},{5,6},{6,7},{7,8},{8,9},{9,10},{10,1... | collective-permute-start | bytes 1179656 | tf_op jit(solution)/shard_map/ppermute | solution.py:13
  307.2 157.8 %collective-permute-start.23 = (f32[384,256]{1,0:T(8,128)}, f32[384,256]{1,0:T(8,128)}, u32[]{:S(2)}, u32[]{:S(2)}) collective-permute-start(f32[384,256]{1,0:T(8,128)} %get-tuple-element.6), channel_id=1, source_target_pairs={{1,0},{2,1},{3,2},{4,3},{5,4},{6,5},{7,6},{8,7},{9,8},{10,9},{11,1... | collective-permute-start | bytes 1179656 | tf_op jit(solution)/shard_map/ppermute | solution.py:13
  308.4 158.2 %collective-permute-start.21 = (f32[384,256]{1,0:T(8,128)}, f32[384,256]{1,0:T(8,128)}, u32[]{:S(2)}, u32[]{:S(2)}) collective-permute-start(f32[384,256]{1,0:T(8,128)} %get-tuple-element.7), channel_id=1, source_target_pairs={{16,0},{32,16},{48,32},{64,48},{80,64},{96,80},{112,96},{17,1},{33... | collective-permute-start | bytes 1179656 | tf_op jit(solution)/shard_map/ppermute | solution.py:13
  (45 other events, 484.8 us)
Sparse Core Ops, SparseCore 0:
  10.8 72.5 all-gather.2
  103.3 147.5 all-reduce.2
  298.4 151.1 all-reduce.4
where the time goes:
time: 486 us; the launch traced here: 480 us
  waiting for transfers between devices  297 us (61%)
  matrix products  78.2 us (16%)
  starting transfers between devices  68.4 us (14%)
  between operations  15.1 us (3%)
  local copies, waits for them, and re-layouts  12.4 us (3%)
  other arithmetic  9.11 us (2%)
    psum x2, waiting for transfers between devices, reduced(): total = lax.psum(jnp.dot(place, block, precision=HIGHEST), ('sx', 'sy'))  273 us
    ppermute x24, starting transfers between devices, shifted(): return lax.ppermute(block, axis, route)  68.1 us
    ppermute x24, waiting for transfers between devices, shifted(): return lax.ppermute(block, axis, route)  23.2 us
    dot_general x20, matrix products, jump(): jnp.dot(match[f], received[f], precision=HIGHEST)  23.1 us
    dot_general x2, matrix products, precondition(): applied = jnp.dot(prec_mat, spread, precision=HIGH)  11.6 us
    dot_general x2, matrix products, coarse(): return (jnp.dot(coupling_jump, sol, precision=HIGHEST), inner(rhs, sol))  10.9 us
    dot_general x2, matrix products, flexible(): jnp.dot(flex_mat, spread, precision=HIGH)  9.93 us
  transfers between devices with their start and end apart: 27, of which 9 were waited for; matrix products, arithmetic and copies ran while one was open for 13% of the time, Pallas kernels for 0%

commit v1 on v0

--- a/solution.py
+++ b/solution.py
@@ -74,7 +74,8 @@
     def reduced(local_load, *rows):
         rows = list(rows) + [jnp.zeros_like(rows[0])] * (3 - len(rows))
         block = jnp.concatenate([local_load] + [row[None] for row in rows], axis=0)
-        total = lax.psum(jnp.dot(place, block, precision=HIGHEST), ("sx", "sy"))
+        mat = jnp.dot(place, block, precision=HIGHEST)
+        total = jax.lax.all_gather(mat, axis_name=("sx", "sy")).sum(axis=0)
         return (total[:ncoarse], total[ncoarse + 1], total[ncoarse + 2], total[ncoarse + 3])
 
     def coarse(rhs):

time: 486 us -> 558 us (1.15)
  other arithmetic: 9.11 us -> 47.4 us
  waiting for transfers between devices: 297 us -> 334 us
    all_gather x0 -> x2, waiting for transfers between devices: none -> 294 us  [reduced(): total = jax.lax.all_gather(mat, axis_name=('sx', 'sy')).sum(axis=0)]
    psum x2 -> x0, waiting for transfers between devices: 273 us -> none  [reduced(): total = lax.psum(jnp.dot(place, block, precision=HIGHEST), ('sx', 'sy'))]
    reduce_sum x2, other arithmetic: 2.87 us -> 43.1 us  [reduced(): total = jax.lax.all_gather(mat, axis_name=('sx', 'sy')).sum(axis=0)]
    ppermute x24, waiting for transfers between devices: 23.2 us -> 39.5 us  [shifted(): return lax.ppermute(block, axis, route)]
  transfers between devices with their start and end apart: 27 -> 27, of which waited for: 9 -> 13; matrix products, arithmetic and copies ran while one was open for 13% -> 9% of each run, Pallas kernels for 0% -> 0%
where the time goes in v1:
time: 558 us; the launch traced here: 551 us
  waiting for transfers between devices  334 us (60%)
  matrix products  75.6 us (14%)
  starting transfers between devices  69.9 us (13%)
  other arithmetic  47.4 us (8%)
  between operations  15.1 us (3%)
  local copies, waits for them, and re-layouts  9.32 us (2%)
    all_gather x2, waiting for transfers between devices, reduced(): total = jax.lax.all_gather(mat, axis_name=('sx', 'sy')).sum(axis=0)  294 us
    ppermute x24, starting transfers between devices, shifted(): return lax.ppermute(block, axis, route)  69.8 us
    reduce_sum x2, other arithmetic, reduced(): total = jax.lax.all_gather(mat, axis_name=('sx', 'sy')).sum(axis=0)  43.1 us
    ppermute x24, waiting for transfers between devices, shifted(): return lax.ppermute(block, axis, route)  39.5 us
    dot_general x20, matrix products, jump(): jnp.dot(match[f], received[f], precision=HIGHEST)  21.1 us
    dot_general x2, matrix products, precondition(): applied = jnp.dot(prec_mat, spread, precision=HIGH)  15.4 us
    dot_general x2, matrix products, coarse(): return (jnp.dot(coupling_jump, sol, precision=HIGHEST), inner(rhs, sol))  11.6 us
  transfers between devices with their start and end apart: 27, of which 13 were waited for; matrix products, arithmetic and copies ran while one was open for 9% of the time, Pallas kernels for 0%

profile of v1, /device:TPU:1, one launch (start us, length us, event | category | flops | bytes accessed | tf_op | source)
XLA Modules:
  0.0 551.1 jit_solution(760302953178114721)
XLA Ops:
  10.8 5.8 %collective-permute-start.2 = (f32[384,256]{1,0:T(8,128)S(1)}, f32[384,256]{1,0:T(8,128)}, u32[]{:S(2)}, u32[]{:S(2)}) collective-permute-start(f32[384,256]{1,0:T(8,128)S(1)} %get-tuple-element.22), channel_id=1, source_target_pairs={{0,1},{1,2},{2,3},{3,4},{4,5},{5,6},{6,7},{7,8},{8,9},{9,10},{10,1... | collective-permute-start | bytes 1179656 | tf_op jit(solution)/shard_map/ppermute | solution.py:13
  30.1 8.0 %multiply_reduce_fusion.4 = (f32[256]{0:T(256)S(1)}, f32[1536,256]{1,0:T(8,128)S(1)}) fusion(f32[1536]{0:T(1024)S(1)} %mul.194, f32[384,256]{1,0:T(8,128)S(1)} %convolution_subtract_fusion.20, f32[384,256]{1,0:T(8,128)S(1)} %convolution_subtract_fusion.21, f32[384,256]{1,0:T(8,128)S(1)} %convolution_subtract_fusion.22, ...), kind=kOutput, calls=%fused_computation.36 | convolution fusion | flops 3627810560 | bytes 12590080 | tf_op jit(solution)/shard_map/dot_general | solution.py:87
  38.3 4.0 collective-permute-start.4
  44.2 3.6 collective-permute-start.6
  55.3 4.1 collective-permute-done.7
  60.6 4.2 multiply_reduce_fusion.3
  67.5 5.3 collective-permute-start.14
  74.7 6.2 %collective-permute-start.12 = (f32[392,16]{0,1:T(8,128)S(1)}, f32[392,16]{0,1:T(8,128)S(1)}, u32[]{:S(2)}, u32[]{:S(2)}) collective-permute-start(f32[392,16]{0,1:T(8,128)S(1)} %get-tuple-element.28), channel_id=1, source_target_pairs={{0,16},{16,32},{32,48},{48,64},{64,80},{80,96},{96,112},{1,17},{17... | collective-permute-start | bytes 75272 | tf_op jit(solution)/shard_map/ppermute | solution.py:13
  95.5 5.6 %collective-permute-start.10 = (f32[384,256]{1,0:T(8,128)S(1)}, f32[384,256]{1,0:T(8,128)S(1)}, u32[]{:S(2)}, u32[]{:S(2)}) collective-permute-start(f32[384,256]{1,0:T(8,128)S(1)} %get-tuple-element.13), channel_id=1, source_target_pairs={{0,1},{1,2},{2,3},{3,4},{4,5},{5,6},{6,7},{7,8},{8,9},{9,10},{10,1... | collective-permute-start | bytes 1179656 | tf_op jit(solution)/shard_map/ppermute | solution.py:13
  105.0 6.7 %collective-permute-done.10 = f32[384,256]{1,0:T(8,128)S(1)} collective-permute-done((f32[384,256]{1,0:T(8,128)S(1)}, f32[384,256]{1,0:T(8,128)S(1)}, u32[]{:S(2)}, u32[]{:S(2)}) %collective-permute-start.10) | collective-permute-done | bytes 393248 | tf_op jit(solution)/shard_map/ppermute | solution.py:13
  113.0 8.0 %collective-permute-done.11 = f32[384,256]{1,0:T(8,128)S(1)} collective-permute-done((f32[384,256]{1,0:T(8,128)S(1)}, f32[384,256]{1,0:T(8,128)S(1)}, u32[]{:S(2)}, u32[]{:S(2)}) %collective-permute-start.11) | collective-permute-done | bytes 393248 | tf_op jit(solution)/shard_map/ppermute | solution.py:13
  123.8 143.3 %all-gather.7.cloned.1.call-done = f32[66560,256]{1,0:T(8,128)} async-done(((f32[520,256]{1,0:T(8,128)}), f32[66560,256]{1,0:T(8,128)}) %all-gather.7.cloned.1.call-update) | async-done | bytes 68157456 | tf_op jit(solution)/shard_map/all_gather | solution.py:78
  267.1 22.0 %reduce_sum.87 = f32[520,256]{1,0:T(8,128)} reduce(f32[128,520,256]{2,1,0:T(8,128)} %bitcast.26, f32[]{:T(128)} %constant.10.clone.1), dimensions={0}, to_apply=%region_2.0 | reduce | flops 16906240 | bytes 68689920 | tf_op jit(solution)/shard_map/reduce_sum | solution.py:78
  297.1 4.9 fusion.9
  302.0 7.4 %multiply_reduce_fusion.2 = (f32[256]{0:T(256)S(1)}, f32[1536,256]{1,0:T(8,128)S(1)}) fusion(f32[1536,256]{1,0:T(8,128)S(1)} %fusion.9, f32[1536]{0:T(1024)S(1)} %mul.194, f32[1,1,1536,1536]{3,2,1,0:T(8,128)} %param.9), kind=kOutput, calls=%fused_computation.34 | convolution fusion | flops 3625451264 | bytes 12590080 | tf_op jit(solution)/shard_map/dot_general | solution.py:87
  309.6 3.4 collective-permute-start.16
  318.5 3.9 collective-permute-done.17
  324.9 3.6 collective-permute-done.19
  329.1 5.8 %multiply_reduce_fusion.1 = (f32[256]{0:T(256)S(1)}, f32[256]{0:T(256)S(1)}, f32[1536,256]{1,0:T(8,128)}) fusion(f32[1536]{0:T(1024)S(1)} %broadcast_multiply_fusion, f32[384,256]{1,0:T(8,128)S(1)} %convolution_subtract_fusion.8, f32[384,256]{1,0:T(8,128)S(1)} %convolution_subtract_fusion.9, f32[384,256]{1,0:T(8,128)S(1)} %convolution_subtract_fusion.10, ...), kind=kOutput, calls=%fused_computation.33 | convolution fusion | flops 3628596736 | bytes 14163968 | tf_op jit(solution)/shard_map/dot_general | solution.py:94
  336.8 4.4 collective-permute-start.20
  354.4 5.3 collective-permute-done.23
  361.0 151.0 %all-gather.9.cloned.1.call-done = f32[66560,256]{1,0:T(8,128)} async-done(((f32[520,256]{1,0:T(8,128)}), f32[66560,256]{1,0:T(8,128)}) %all-gather.9.cloned.1.call-update) | async-done | bytes 68157456 | tf_op jit(solution)/shard_map/all_gather | solution.py:78
  512.0 21.1 %reduce_sum.93 = f32[520,256]{1,0:T(8,128)S(1)} reduce(f32[128,520,256]{2,1,0:T(8,128)} %bitcast.45, f32[]{:T(128)} %constant.10.clone.1), dimensions={0}, to_apply=%region_7.0 | reduce | flops 16906240 | bytes 68689920 | tf_op jit(solution)/shard_map/reduce_sum | solution.py:78
  536.2 6.7 %fusion.29 = f32[1,1,1536,256]{3,2,1,0:T(8,128)} fusion(f32[1536,256]{1,0:T(8,128)S(1)} %copy-done.28, f32[384,256]{1,0:T(8,128)} %convolution_subtract_fusion.4, f32[384,256]{1,0:T(8,128)} %convolution_subtract_fusion.5, f32[384,256]{1,0:T(8,128)} %convolution_subtract_fusion.6, f32[384,256]{1,0:T(8,128)} %convolution_subtract_fusion.7, ...), kind=kOutput, calls=%fused_computation.31 | convolution fusion | flops 2422603776 | bytes 9963520 | tf_op jit(solution)/shard_map/dot_general | solution.py:83
  (195 shorter events, 92.1 us)
Async XLA Ops:
  7.2 115.1 %all-gather.11.cloned.1.call-start = ((), (), s32[]{:S(2)}) async-start(), calls=%async_computation.2 | async-start | bytes 1056768 | tf_op jit(solution)/shard_map/all_gather | solution.py:54
  9.5 14.0 %collective-permute-start.3 = (f32[384,256]{1,0:T(8,128)}, f32[384,256]{1,0:T(8,128)}, u32[]{:S(2)}, u32[]{:S(2)}) collective-permute-start(f32[384,256]{1,0:T(8,128)} %get-tuple-element.23), channel_id=1, source_target_pairs={{1,0},{2,1},{3,2},{4,3},{5,4},{6,5},{7,6},{8,7},{9,8},{10,9},{11,1... | collective-permute-start | bytes 1179656 | tf_op jit(solution)/shard_map/ppermute | solution.py:13
  10.8 14.3 %collective-permute-start.2 = (f32[384,256]{1,0:T(8,128)S(1)}, f32[384,256]{1,0:T(8,128)}, u32[]{:S(2)}, u32[]{:S(2)}) collective-permute-start(f32[384,256]{1,0:T(8,128)S(1)} %get-tuple-element.22), channel_id=1, source_target_pairs={{0,1},{1,2},{2,3},{3,4},{4,5},{5,6},{6,7},{7,8},{8,9},{9,10},{10,1... | collective-permute-start | bytes 1179656 | tf_op jit(solution)/shard_map/ppermute | solution.py:13
  16.6 10.1 %collective-permute-start.1 = (f32[384,256]{1,0:T(8,128)S(1)}, f32[384,256]{1,0:T(8,128)}, u32[]{:S(2)}, u32[]{:S(2)}) collective-permute-start(f32[384,256]{1,0:T(8,128)S(1)} %get-tuple-element.21), channel_id=1, source_target_pairs={{16,0},{32,16},{48,32},{64,48},{80,64},{96,80},{112,96},{17,1},{33... | collective-permute-start | bytes 1179656 | tf_op jit(solution)/shard_map/ppermute | solution.py:13
  22.7 244.4 %all-gather.7.cloned.1.call-start = ((), (), s32[]{:S(2)}) async-start(), calls=%async_computation | async-start | bytes 68689920 | tf_op jit(solution)/shard_map/all_gather | solution.py:78
  38.3 11.4 %collective-permute-start.4 = (f32[384,256]{1,0:T(8,128)S(1)}, f32[384,256]{1,0:T(8,128)S(1)}, u32[]{:S(2)}, u32[]{:S(2)}) collective-permute-start(f32[384,256]{1,0:T(8,128)S(1)} %get-tuple-element.16), channel_id=1, source_target_pairs={{0,16},{16,32},{32,48},{48,64},{64,80},{80,96},{96,112},{1,17},{17... | collective-permute-start | bytes 1179656 | tf_op jit(solution)/shard_map/ppermute | solution.py:13
  42.3 9.4 %collective-permute-start.5 = (f32[384,256]{1,0:T(8,128)S(1)}, f32[384,256]{1,0:T(8,128)S(1)}, u32[]{:S(2)}, u32[]{:S(2)}) collective-permute-start(f32[384,256]{1,0:T(8,128)S(1)} %get-tuple-element.19), channel_id=1, source_target_pairs={{16,0},{32,16},{48,32},{64,48},{80,64},{96,80},{112,96},{17,1},{33... | collective-permute-start | bytes 1179656 | tf_op jit(solution)/shard_map/ppermute | solution.py:13
  44.2 10.5 %collective-permute-start.6 = (f32[384,256]{1,0:T(8,128)S(1)}, f32[384,256]{1,0:T(8,128)S(1)}, u32[]{:S(2)}, u32[]{:S(2)}) collective-permute-start(f32[384,256]{1,0:T(8,128)S(1)} %get-tuple-element.17), channel_id=1, source_target_pairs={{0,1},{1,2},{2,3},{3,4},{4,5},{5,6},{6,7},{7,8},{8,9},{9,10},{10,1... | collective-permute-start | bytes 1179656 | tf_op jit(solution)/shard_map/ppermute | solution.py:13
  47.8 11.6 %collective-permute-start.7 = (f32[384,256]{1,0:T(8,128)S(1)}, f32[384,256]{1,0:T(8,128)S(1)}, u32[]{:S(2)}, u32[]{:S(2)}) collective-permute-start(f32[384,256]{1,0:T(8,128)S(1)} %get-tuple-element.18), channel_id=1, source_target_pairs={{1,0},{2,1},{3,2},{4,3},{5,4},{6,5},{7,6},{8,7},{9,8},{10,9},{11,1... | collective-permute-start | bytes 1179656 | tf_op jit(solution)/shard_map/ppermute | solution.py:13
  66.0 446.0 %all-gather.9.cloned.1.call-start = ((), (), s32[]{:S(2)}) async-start(), calls=%async_computation.1 | async-start | bytes 68689920 | tf_op jit(solution)/shard_map/all_gather | solution.py:78
  66.2 16.8 %collective-permute-start.15 = (f32[392,16]{0,1:T(8,128)S(1)}, f32[392,16]{0,1:T(8,128)S(1)}, u32[]{:S(2)}, u32[]{:S(2)}) collective-permute-start(f32[392,16]{0,1:T(8,128)S(1)} %get-tuple-element.31), channel_id=1, source_target_pairs={{1,0},{2,1},{3,2},{4,3},{5,4},{6,5},{7,6},{8,7},{9,8},{10,9},{11,1... | collective-permute-start | bytes 75272 | tf_op jit(solution)/shard_map/ppermute | solution.py:13
  67.5 15.7 %collective-permute-start.14 = (f32[392,16]{0,1:T(8,128)S(1)}, f32[392,16]{0,1:T(8,128)S(1)}, u32[]{:S(2)}, u32[]{:S(2)}) collective-permute-start(f32[392,16]{0,1:T(8,128)S(1)} %get-tuple-element.30), channel_id=1, source_target_pairs={{0,1},{1,2},{2,3},{3,4},{4,5},{5,6},{6,7},{7,8},{8,9},{9,10},{10,1... | collective-permute-start | bytes 75272 | tf_op jit(solution)/shard_map/ppermute | solution.py:13
  72.8 10.5 %collective-permute-start.13 = (f32[392,16]{0,1:T(8,128)S(1)}, f32[392,16]{0,1:T(8,128)S(1)}, u32[]{:S(2)}, u32[]{:S(2)}) collective-permute-start(f32[392,16]{0,1:T(8,128)S(1)} %get-tuple-element.29), channel_id=1, source_target_pairs={{16,0},{32,16},{48,32},{64,48},{80,64},{96,80},{112,96},{17,1},{33... | collective-permute-start | bytes 75272 | tf_op jit(solution)/shard_map/ppermute | solution.py:13
  74.7 16.7 %collective-permute-start.12 = (f32[392,16]{0,1:T(8,128)S(1)}, f32[392,16]{0,1:T(8,128)S(1)}, u32[]{:S(2)}, u32[]{:S(2)}) collective-permute-start(f32[392,16]{0,1:T(8,128)S(1)} %get-tuple-element.28), channel_id=1, source_target_pairs={{0,16},{16,32},{32,48},{48,64},{64,80},{80,96},{96,112},{1,17},{17... | collective-permute-start | bytes 75272 | tf_op jit(solution)/shard_map/ppermute | solution.py:13
  89.1 13.3 %collective-permute-start.8 = (f32[384,256]{1,0:T(8,128)S(1)}, f32[384,256]{1,0:T(8,128)S(1)}, u32[]{:S(2)}, u32[]{:S(2)}) collective-permute-start(f32[384,256]{1,0:T(8,128)S(1)} %get-tuple-element.12), channel_id=1, source_target_pairs={{0,16},{16,32},{32,48},{48,64},{64,80},{80,96},{96,112},{1,17},{17... | collective-permute-start | bytes 1179656 | tf_op jit(solution)/shard_map/ppermute | solution.py:13
  92.0 11.7 %collective-permute-start.9 = (f32[384,256]{1,0:T(8,128)S(1)}, f32[384,256]{1,0:T(8,128)S(1)}, u32[]{:S(2)}, u32[]{:S(2)}) collective-permute-start(f32[384,256]{1,0:T(8,128)S(1)} %get-tuple-element.15), channel_id=1, source_target_pairs={{16,0},{32,16},{48,32},{64,48},{80,64},{96,80},{112,96},{17,1},{33... | collective-permute-start | bytes 1179656 | tf_op jit(solution)/shard_map/ppermute | solution.py:13
  95.5 16.2 %collective-permute-start.10 = (f32[384,256]{1,0:T(8,128)S(1)}, f32[384,256]{1,0:T(8,128)S(1)}, u32[]{:S(2)}, u32[]{:S(2)}) collective-permute-start(f32[384,256]{1,0:T(8,128)S(1)} %get-tuple-element.13), channel_id=1, source_target_pairs={{0,1},{1,2},{2,3},{3,4},{4,5},{5,6},{6,7},{7,8},{8,9},{9,10},{10,1... | collective-permute-start | bytes 1179656 | tf_op jit(solution)/shard_map/ppermute | solution.py:13
  101.1 19.9 %collective-permute-start.11 = (f32[384,256]{1,0:T(8,128)S(1)}, f32[384,256]{1,0:T(8,128)S(1)}, u32[]{:S(2)}, u32[]{:S(2)}) collective-permute-start(f32[384,256]{1,0:T(8,128)S(1)} %get-tuple-element.14), channel_id=1, source_target_pairs={{1,0},{2,1},{3,2},{4,3},{5,4},{6,5},{7,6},{8,7},{9,8},{10,9},{11,1... | collective-permute-start | bytes 1179656 | tf_op jit(solution)/shard_map/ppermute | solution.py:13
  313.0 9.4 %collective-permute-start.17 = (f32[384,256]{1,0:T(8,128)S(1)}, f32[384,256]{1,0:T(8,128)S(1)}, u32[]{:S(2)}, u32[]{:S(2)}) collective-permute-start(f32[384,256]{1,0:T(8,128)S(1)} %get-tuple-element.11), channel_id=1, source_target_pairs={{16,0},{32,16},{48,32},{64,48},{80,64},{96,80},{112,96},{17,1},{33... | collective-permute-start | bytes 1179656 | tf_op jit(solution)/shard_map/ppermute | solution.py:13
  314.9 9.4 %collective-permute-start.18 = (f32[384,256]{1,0:T(8,128)S(1)}, f32[384,256]{1,0:T(8,128)S(1)}, u32[]{:S(2)}, u32[]{:S(2)}) collective-permute-start(f32[384,256]{1,0:T(8,128)S(1)} %get-tuple-element.9), channel_id=1, source_target_pairs={{0,1},{1,2},{2,3},{3,4},{4,5},{5,6},{6,7},{7,8},{8,9},{9,10},{10,1... | collective-permute-start | bytes 1179656 | tf_op jit(solution)/shard_map/ppermute | solution.py:13
  316.4 12.0 %collective-permute-start.19 = (f32[384,256]{1,0:T(8,128)S(1)}, f32[384,256]{1,0:T(8,128)S(1)}, u32[]{:S(2)}, u32[]{:S(2)}) collective-permute-start(f32[384,256]{1,0:T(8,128)S(1)} %get-tuple-element.10), channel_id=1, source_target_pairs={{1,0},{2,1},{3,2},{4,3},{5,4},{6,5},{7,6},{8,7},{9,8},{10,9},{11,1... | collective-permute-start | bytes 1179656 | tf_op jit(solution)/shard_map/ppermute | solution.py:13
  336.8 11.1 %collective-permute-start.20 = (f32[384,256]{1,0:T(8,128)S(1)}, f32[384,256]{1,0:T(8,128)S(1)}, u32[]{:S(2)}, u32[]{:S(2)}) collective-permute-start(f32[384,256]{1,0:T(8,128)S(1)} %get-tuple-element.4), channel_id=1, source_target_pairs={{0,16},{16,32},{32,48},{48,64},{64,80},{80,96},{96,112},{1,17},{17... | collective-permute-start | bytes 1179656 | tf_op jit(solution)/shard_map/ppermute | solution.py:13
  343.1 10.0 %collective-permute-start.22 = (f32[384,256]{1,0:T(8,128)S(1)}, f32[384,256]{1,0:T(8,128)S(1)}, u32[]{:S(2)}, u32[]{:S(2)}) collective-permute-start(f32[384,256]{1,0:T(8,128)S(1)} %get-tuple-element.5), channel_id=1, source_target_pairs={{0,1},{1,2},{2,3},{3,4},{4,5},{5,6},{6,7},{7,8},{8,9},{9,10},{10,1... | collective-permute-start | bytes 1179656 | tf_op jit(solution)/shard_map/ppermute | solution.py:13
  346.3 13.3 %collective-permute-start.23 = (f32[384,256]{1,0:T(8,128)S(1)}, f32[384,256]{1,0:T(8,128)S(1)}, u32[]{:S(2)}, u32[]{:S(2)}) collective-permute-start(f32[384,256]{1,0:T(8,128)S(1)} %get-tuple-element.6), channel_id=1, source_target_pairs={{1,0},{2,1},{3,2},{4,3},{5,4},{6,5},{7,6},{8,7},{9,8},{10,9},{11,1... | collective-permute-start | bytes 1179656 | tf_op jit(solution)/shard_map/ppermute | solution.py:13
  (43 other events, 434.9 us)
Sparse Core Ops, SparseCore 0:
  22.8 72.3 all-gather.10
  98.7 168.3 all-gather.6
  336.8 175.1 all-gather.8
